TPU v7x, 32 devices: a whole 2x2x4 slice. The times are simulated.
32 devices in a mesh: row: 8 (over y, x, core), col: 4 (over z).
Axes of the slice: x: 2, y: 2, z: 4, core: 2. Of those that a mesh axis runs over, the one named last changes fastest.
Arguments:
- right_sides: float32 [64, 32768], P(None, ('row', 'col'))
- diag_tiles: float32 [32, 1024, 1024], P(('row', 'col')), as said below
- low_rank: float32 [32, 4, 8, 2, 12, 1024], P('row', 'col'), as said below
- tile_ranks: int32 [32, 4, 8], P('row', 'col'), may hold values from 1 to 12, as said below
- inv_factor: float32 [256, 8, 128, 128], P(('row', 'col')), as said below
- sub_sizes: int32 [64], replicated, may hold values from 1 to 8, 256 in all
Outputs:
- solution: float32 [64, 32768], P(None, ('row', 'col'))
- residual: float32 [64, 32768], P(None, ('row', 'col'))
Inputs may be any that keep to these rules, and one draw needn't show every extreme that they name: `low_rank`: tile (j, i) holds the two factors of tile (i, j) in swapped order, and a diagonal tile's two factors are equal, so S is symmetric. `tile_ranks`: the rank of tile (i, j) equals that of tile (j, i); diagonal tiles have rank 12. `diag_tiles`: each tile is symmetric positive definite. `inv_factor`: the block at distance 0 of every span is lower triangular with a positive diagonal. `sub_sizes`: the sizes sum to 256.
All inputs are finite; a program needn't handle non-finite values.
Results may differ from a plain program's by a relative error of at most 0.0003.
Values sent between devices are 32-bit elements; how exact they have to be, the bound alone decides.
A program may use at most 128 MiB of HBM per device.

v0:
```python
import jax
import jax.numpy as jnp
from jax import lax
from jax.sharding import PartitionSpec as P

RANK = 12


finest = lax.Precision.HIGHEST


def shifted(x, axis, by):
    size = lax.axis_size(axis)
    pairs = [(i, i + by) for i in range(size) if 0 <= i + by < size]
    return lax.ppermute(x, axis, pairs)


def span_weights(sub_sizes, per_device, reach_len):
    span_ids = lax.axis_index(("row", "col")) * per_device + lax.iota(jnp.int32, per_device)
    ending = jnp.cumsum(sub_sizes)
    opening = ending - sub_sizes
    inside = (span_ids[:, None] >= opening[None, :]) & (span_ids[:, None] < ending[None, :])
    position = span_ids - jnp.sum(jnp.where(inside, opening[None, :], 0), axis=1)
    return (lax.iota(jnp.int32, reach_len)[None, :] <= position[:, None]).astype(jnp.float32)


def precondition(vector, inv_factor, weights):
    rhs_count, tile_len = vector.shape
    per_device = inv_factor.shape[0]
    reach_len = inv_factor.shape[1]
    span_len = inv_factor.shape[2]
    before = shifted(vector, ("row", "col"), 1)
    joined = jnp.concatenate([before, vector], axis=1).reshape(rhs_count, 2 * per_device, span_len)
    windows = jnp.stack(
        [joined[:, per_device - behind : 2 * per_device - behind] for behind in range(reach_len)],
        axis=2,
    )
    windows = windows * weights[None, :, :, None]
    forward = jnp.einsum("ltji,klti->klj", inv_factor, windows, precision=finest)
    spread = (
        jnp.einsum("ltji,klj->klti", inv_factor, forward, precision=finest)
        * weights[None, :, :, None]
    )
    placed = jnp.zeros_like(joined)
    for behind in range(reach_len):
        placed = placed + jnp.pad(
            spread[:, :, behind], ((0, 0), (per_device - behind, behind), (0, 0))
        )
    returned = shifted(placed[:, :per_device].reshape(rhs_count, tile_len), ("row", "col"), -1)
    return placed[:, per_device:].reshape(rhs_count, tile_len) + returned


def operate(vector, diag_tiles, low_rank, tile_ranks):
    rhs_count, tile_len = vector.shape
    tile_rows = low_rank.shape[0]
    local_part = jnp.dot(vector, diag_tiles[0], precision=finest)
    left_factor = low_rank[:, 0, :, 0]
    right_factor = low_rank[:, 0, :, 1]
    weights = (lax.iota(jnp.int32, RANK)[None, None, :] < tile_ranks[:, 0, :, None]).astype(
        jnp.float32
    )
    initial = jnp.zeros((rhs_count, tile_rows * tile_len), jnp.float32)
    piece = lax.all_gather(vector, "row", axis=1, tiled=True)
    count_tiles = piece.shape[1] // tile_len
    pieces = piece.reshape(rhs_count, count_tiles, tile_len)
    coeffs = (
        jnp.einsum("bmqt,pmt->bmqp", right_factor, pieces, precision=finest)
        * weights[:, :, :, None]
    )
    added = jnp.einsum("bmqt,bmqp->pbt", left_factor, coeffs, precision=finest)
    partial_rows = initial + added.reshape(rhs_count, tile_rows * tile_len)
    summed = lax.psum_scatter(partial_rows, "col", scatter_dimension=1, tiled=True)
    return local_part + summed


def solve_spd(matrix, target):
    factor = jnp.linalg.cholesky(matrix)
    return jax.scipy.linalg.cho_solve((factor, True), target)


def gram_of(first_block, second_block):
    return jnp.dot(first_block, second_block.T, precision=finest)


def apply_coeffs(coeffs, block_rows):
    return jnp.dot(coeffs.T, block_rows, precision=finest)


def global_sum(terms):
    return lax.psum((terms[0], terms[1]), ("row", "col"))


def body(right_sides, diag_tiles, low_rank, tile_ranks, inv_factor, sub_sizes):
    weights = span_weights(sub_sizes, inv_factor.shape[0], inv_factor.shape[1])
    residual = right_sides
    search = precondition(residual, inv_factor, weights)
    images = operate(search, diag_tiles, low_rank, tile_ranks)
    rho_now, curvature = global_sum((gram_of(search, residual), gram_of(search, images)))
    step_size = solve_spd(curvature, rho_now)
    solution = apply_coeffs(step_size, search)
    residual = residual - apply_coeffs(step_size, images)
    precond = precondition(residual, inv_factor, weights)
    product = operate(precond, diag_tiles, low_rank, tile_ranks)
    rho_next, self_term, cross_term = lax.psum(
        (gram_of(precond, residual), gram_of(precond, product), gram_of(search, product)),
        ("row", "col"),
    )
    beta_mix = solve_spd(rho_now, rho_next)
    curvature = (
        self_term
        + jnp.dot(cross_term.T, beta_mix, precision=finest)
        + jnp.dot(beta_mix.T, cross_term, precision=finest)
        + jnp.dot(beta_mix.T, jnp.dot(curvature, beta_mix, precision=finest), precision=finest)
    )
    search = precond + apply_coeffs(beta_mix, search)
    images = product + apply_coeffs(beta_mix, images)
    step_size = solve_spd(curvature, rho_next)
    solution = solution + apply_coeffs(step_size, search)
    residual = residual - apply_coeffs(step_size, images)
    return (solution, residual)


def solution(mesh):
    placed = (
        P(None, ("row", "col")),
        P(("row", "col"), None, None),
        P("row", "col", None, None, None, None),
        P("row", "col", None),
        P(("row", "col"), None, None, None),
        P(),
    )
    return jax.shard_map(
        body,
        mesh=mesh,
        in_specs=placed,
        out_specs=(P(None, ("row", "col")), P(None, ("row", "col"))),
        check_vma=False,
    )
```

profile of v0, /device:TPU:0, one launch (start us, length us, event | category | flops | bytes accessed | tf_op | source)
XLA Modules:
  0.0 334.7 jit_solution(9789738542311892284)
XLA Ops:
  7.2 5.0 %collective-permute-start = (f32[64,1024]{1,0:T(8,128)}, f32[64,1024]{1,0:T(8,128)S(1)}, u32[]{:S(2)}, u32[]{:S(2)}) collective-permute-start(f32[64,1024]{1,0:T(8,128)} %param.9), channel_id=1, source_target_pairs={{0,1},{1,2},{2,3},{3,4},{4,5},{5,6},{6,7},{7,8},{8,9},{9,10},{10,1... | collective-permute-start | bytes 786440 | tf_op jit(solution)/shard_map/ppermute | solution.py:15
  14.1 3.9 %collective-permute-done = f32[64,1024]{1,0:T(8,128)S(1)} collective-permute-done((f32[64,1024]{1,0:T(8,128)}, f32[64,1024]{1,0:T(8,128)S(1)}, u32[]{:S(2)}, u32[]{:S(2)}) %collective-permute-start) | collective-permute-done | bytes 262176 | tf_op jit(solution)/shard_map/ppermute | solution.py:15
  21.5 4.6 %fusion.20 = f32[64,8,128,1]{2,0,3,1:T(8,128)S(1)} fusion(f32[8,8,128,128]{3,2,1,0:T(8,128)S(1)} %copy-done, f32[64,8,8,128]{3,0,2,1:T(8,128)S(1)} %fusion.62, f32[8,8]{1,0:T(8,128)S(1)} %fusion.89), kind=kOutput, calls=%fused_computation.23 | convolution fusion | flops 805830656 | bytes 6553856 | tf_op jit(solution)/shard_map/ltji,klti->klj/dot_general | solution.py:39
  30.3 8.7 %collective-permute-done.1 = f32[64,1024]{1,0:T(8,128)S(1)} collective-permute-done((f32[64,1024]{1,0:T(8,128)S(1)}, f32[64,1024]{1,0:T(8,128)S(1)}, u32[]{:S(2)}, u32[]{:S(2)}) %collective-permute-start.1) | collective-permute-done | bytes 262176 | tf_op jit(solution)/shard_map/ppermute | solution.py:15
  40.2 6.1 %fusion.91 = (f32[4,1,8,1,12,1024]{5,3,4,2,1,0:T(1,128)S(1)}, f32[4,1,8,1,12,1024]{5,3,4,2,1,0:T(1,128)S(1)}) fusion(f32[4,1,8,2,12,1024]{5,3,4,2,1,0:T(2,128)} %param.11), kind=kLoop, calls=%fused_computation.139 | loop fusion | bytes 6291456 | tf_op jit(solution)/shard_map/slice | solution.py:57
  46.3 25.4 %all-gather.3.cloned.1.call-done = f32[64,8192]{1,0:T(8,128)} async-done(((f32[64,1024]{1,0:T(8,128)}), f32[64,8192]{1,0:T(8,128)}) %all-gather.3.cloned.1.call-update) | async-done | bytes 2097168 | tf_op jit(solution)/shard_map/all_gather | solution.py:63
  82.5 25.7 %reduce-scatter.3.cloned.1.call-done = f32[64,1024]{1,0:T(8,128)} async-done(((f32[64,4096]{1,0:T(8,128)}), f32[64,1024]{1,0:T(8,128)}) %reduce-scatter.3.cloned.1.call-update) | async-done | bytes 262160 | tf_op jit(solution)/shard_map/reduce_scatter | solution.py:72
  108.2 4.9 %fusion.26 = f32[64,1024]{1,0:T(8,128)S(1)} fusion(f32[64,1024]{1,0:T(8,128)} %reduce-scatter.3.cloned.1.call-done, f32[64,1024]{1,0:T(8,128)S(1)} %copy-done.2, f32[1,1024,1024]{2,1,0:T(8,128)} %param.10), kind=kOutput, calls=%fused_computation.25 | convolution fusion | flops 805371904 | bytes 4980736 | tf_op jit(solution)/shard_map/dot_general | solution.py:56
  114.1 39.2 %all-reduce.17 = (f32[64,64]{0,1:T(8,128)S(1)}, f32[64,64]{0,1:T(8,128)S(1)}) all-reduce(f32[64,64]{0,1:T(8,128)S(1)} %fusion.95, f32[64,64]{0,1:T(8,128)S(1)} %fusion.94), channel_id=1, replica_groups=mesh['row'=8,'col'=4] {'row','col'}, use_global_device_ids=true, to_apply=%region_6.8 | all-reduce | flops 8192 | bytes 65536 | tf_op jit(solution)/shard_map/psum | solution.py:90
  153.4 5.8 %cholesky.59 = f32[64,64]{1,0:T(8,128)S(1)} custom-call(f32[64,64]{1,0:T(8,128)S(1)} %fusion.87), custom_call_target="Cholesky" | custom-call | tf_op jit(solution)/shard_map/jit(cholesky)/cholesky | solution.py:77
  161.4 5.7 %custom-call.9 = f32[1,64,64]{1,2,0:T(8,128)S(1)} custom-call(f32[1,64,64]{2,1,0:T(8,128)} %fusion.70), custom_call_target="InvertDiagBlocksLowerTriangular" | custom-call | tf_op jit(solution)/shard_map/jit(_cho_solve)/triangular_solve | solution.py:78
  168.9 3.8 %collective-permute-start.2 = (f32[64,1024]{1,0:T(8,128)S(1)}, f32[64,1024]{1,0:T(8,128)S(1)}, u32[]{:S(2)}, u32[]{:S(2)}) collective-permute-start(f32[64,1024]{1,0:T(8,128)S(1)} %convolution_subtract_fusion.1), channel_id=1, source_target_pairs={{0,1},{1,2},{2,3},{3,4},{4,5},{5,6},{6,7},{7,8},{8,9},{9,10},{10,1... | collective-permute-start | bytes 786440 | tf_op jit(solution)/shard_map/ppermute | solution.py:15
  172.7 4.7 %collective-permute-done.2 = f32[64,1024]{1,0:T(8,128)S(1)} collective-permute-done((f32[64,1024]{1,0:T(8,128)S(1)}, f32[64,1024]{1,0:T(8,128)S(1)}, u32[]{:S(2)}, u32[]{:S(2)}) %collective-permute-start.2) | collective-permute-done | bytes 262176 | tf_op jit(solution)/shard_map/ppermute | solution.py:15
  179.9 4.6 %fusion.23 = f32[64,8,128,1]{2,0,3,1:T(8,128)S(1)} fusion(f32[8,8,128,128]{3,2,1,0:T(8,128)S(1)} %copy-done.1, f32[64,8,8,128]{3,0,2,1:T(8,128)S(1)} %fusion.54, f32[8,8]{1,0:T(8,128)S(1)} %copy-done.9), kind=kOutput, calls=%fused_computation.24 | convolution fusion | flops 805830656 | bytes 6553856 | tf_op jit(solution)/shard_map/ltji,klti->klj/dot_general | solution.py:39
  188.7 9.1 %collective-permute-done.3 = f32[64,1024]{1,0:T(8,128)S(1)} collective-permute-done((f32[64,1024]{1,0:T(8,128)S(1)}, f32[64,1024]{1,0:T(8,128)S(1)}, u32[]{:S(2)}, u32[]{:S(2)}) %collective-permute-start.3) | collective-permute-done | bytes 262176 | tf_op jit(solution)/shard_map/ppermute | solution.py:15
  198.8 29.5 %all-gather.5.cloned.1.call-done = f32[64,8192]{1,0:T(8,128)} async-done(((f32[64,1024]{1,0:T(8,128)}), f32[64,8192]{1,0:T(8,128)}) %all-gather.5.cloned.1.call-update) | async-done | bytes 2097168 | tf_op jit(solution)/shard_map/all_gather | solution.py:63
  231.0 3.6 %fusion.47 = f32[4,8,12,64]{3,2,0,1:T(8,128)S(1)} fusion(f32[4,1,8,1,12,1024]{5,3,4,2,1,0:T(1,128)S(1)} %get-tuple-element.10, f32[64,8,1024,1]{2,1,0,3:T(8,128)S(1)} %bitcast.312, f32[4,8,12]{2,0,1:T(4,128)S(1)} %fusion.88), kind=kOutput, calls=%fused_computation.35 | convolution fusion | flops 302014464 | bytes 3769856 | tf_op jit(solution)/shard_map/bmqt,pmt->bmqp/dot_general | solution.py:67
  237.4 5.8 %cholesky.70 = f32[64,64]{1,0:T(8,128)S(1)} custom-call(f32[64,64]{1,0:T(8,128)S(1)} %fusion.82), custom_call_target="Cholesky" | custom-call | tf_op jit(solution)/shard_map/jit(cholesky)/cholesky | solution.py:77
  244.6 4.9 %custom-call.10 = f32[1,64,64]{1,2,0:T(8,128)S(1)} custom-call(f32[1,64,64]{2,1,0:T(8,128)S(1)} %fusion.71), custom_call_target="InvertDiagBlocksLowerTriangular" | custom-call | tf_op jit(solution)/shard_map/jit(_cho_solve)/triangular_solve | solution.py:78
  249.9 15.0 %reduce-scatter.5.cloned.1.call-done = f32[64,1024]{1,0:T(8,128)} async-done(((f32[64,4096]{1,0:T(8,128)}), f32[64,1024]{1,0:T(8,128)}) %reduce-scatter.5.cloned.1.call-update) | async-done | bytes 262160 | tf_op jit(solution)/shard_map/reduce_scatter | solution.py:72
  264.8 4.8 %fusion.29 = f32[64,1024]{1,0:T(8,128)S(1)} fusion(f32[64,1024]{1,0:T(8,128)} %reduce-scatter.5.cloned.1.call-done, f32[64,1024]{1,0:T(8,128)S(1)} %copy-done.3, f32[1,1024,1024]{2,1,0:T(8,128)} %param.10), kind=kOutput, calls=%fused_computation.26 | convolution fusion | flops 805371904 | bytes 4980736 | tf_op jit(solution)/shard_map/dot_general | solution.py:56
  270.4 40.0 %all-reduce.16 = (f32[64,64]{1,0:T(8,128)S(1)}, f32[64,64]{1,0:T(8,128)S(1)}, f32[64,64]{0,1:T(8,128)S(1)}) all-reduce(f32[64,64]{1,0:T(8,128)S(1)} %fusion.98, f32[64,64]{1,0:T(8,128)S(1)} %fusion.97, f32[64,64]{0,1:T(8,128)S(1)} %fusion.96), channel_id=1, replica_groups=mesh['row'=8,'col'=4] {'row','col'}, use_global_device_ids=true, to_apply=%region_10.13 | all-reduce | flops 12288 | bytes 98304 | tf_op jit(solution)/shard_map/psum | solution.py:104
  312.8 5.8 %cholesky.81 = f32[64,64]{1,0:T(8,128)S(1)} custom-call(f32[64,64]{1,0:T(8,128)S(1)} %fusion.77), custom_call_target="Cholesky" | custom-call | tf_op jit(solution)/shard_map/jit(cholesky)/cholesky | solution.py:77
  320.0 4.9 %custom-call.11 = f32[1,64,64]{1,2,0:T(8,128)S(1)} custom-call(f32[1,64,64]{2,1,0:T(8,128)S(1)} %fusion.72), custom_call_target="InvertDiagBlocksLowerTriangular" | custom-call | tf_op jit(solution)/shard_map/jit(_cho_solve)/triangular_solve | solution.py:78
  (119 shorter events, 48.5 us)
Async XLA Ops:
  7.2 64.6 %all-gather.3.cloned.1.call-start = ((), (), s32[]{:S(2)}) async-start(), calls=%async_computation.2 | async-start | bytes 2359296 | tf_op jit(solution)/shard_map/all_gather | solution.py:63
  7.2 10.8 %collective-permute-start = (f32[64,1024]{1,0:T(8,128)}, f32[64,1024]{1,0:T(8,128)S(1)}, u32[]{:S(2)}, u32[]{:S(2)}) collective-permute-start(f32[64,1024]{1,0:T(8,128)} %param.9), channel_id=1, source_target_pairs={{0,1},{1,2},{2,3},{3,4},{4,5},{5,6},{6,7},{7,8},{8,9},{9,10},{10,1... | collective-permute-start | bytes 786440 | tf_op jit(solution)/shard_map/ppermute | solution.py:15
  14.1 12.0 %copy-start.8 = (f32[8,8]{1,0:T(8,128)}, f32[8,8]{1,0:T(8,128)S(1)}, u32[]{:S(2)}) copy-start(f32[8,8]{1,0:T(8,128)S(1)} %fusion.89) | copy-start | bytes 772
  19.3 2.2 copy-start
  28.7 11.3 %copy-start.10 = (s32[4,1,8]{2,1,0:T(1,128)S(1)}, s32[4,1,8]{2,1,0:T(1,128)}, u32[]{:S(2)}) copy-start(s32[4,1,8]{2,1,0:T(1,128)} %param.12) | copy-start | bytes 388
  29.0 10.0 %collective-permute-start.1 = (f32[64,1024]{1,0:T(8,128)S(1)}, f32[64,1024]{1,0:T(8,128)S(1)}, u32[]{:S(2)}, u32[]{:S(2)}) collective-permute-start(f32[64,1024]{1,0:T(8,128)S(1)} %bitcast.318), channel_id=1, source_target_pairs={{1,0},{2,1},{3,2},{4,3},{5,4},{6,5},{7,6},{8,7},{9,8},{10,9},{11,1... | collective-permute-start | bytes 786440 | tf_op jit(solution)/shard_map/ppermute | solution.py:15
  39.8 68.4 %reduce-scatter.3.cloned.1.call-start = ((), (), s32[]{:S(2)}) async-start(), calls=%async_computation.3 | async-start | bytes 1310720 | tf_op jit(solution)/shard_map/reduce_scatter | solution.py:72
  79.7 1.6 copy-start.2
  80.8 147.5 %all-gather.5.cloned.1.call-start = ((), (), s32[]{:S(2)}) async-start(), calls=%async_computation.4 | async-start | bytes 2359296 | tf_op jit(solution)/shard_map/all_gather | solution.py:63
  113.1 0.7 copy-start.4
  168.9 8.6 %copy-start.6 = (f32[64,1024]{1,0:T(8,128)}, f32[64,1024]{1,0:T(8,128)S(1)}, u32[]{:S(2)}) copy-start(f32[64,1024]{1,0:T(8,128)S(1)} %convolution_subtract_fusion.1) | copy-start | bytes 786436
  168.9 8.6 %collective-permute-start.2 = (f32[64,1024]{1,0:T(8,128)S(1)}, f32[64,1024]{1,0:T(8,128)S(1)}, u32[]{:S(2)}, u32[]{:S(2)}) collective-permute-start(f32[64,1024]{1,0:T(8,128)S(1)} %convolution_subtract_fusion.1), channel_id=1, source_target_pairs={{0,1},{1,2},{2,3},{3,4},{4,5},{5,6},{6,7},{7,8},{8,9},{9,10},{10,1... | collective-permute-start | bytes 786440 | tf_op jit(solution)/shard_map/ppermute | solution.py:15
  177.7 2.2 copy-start.1
  177.8 2.2 copy-start.9
  187.4 10.4 %collective-permute-start.3 = (f32[64,1024]{1,0:T(8,128)S(1)}, f32[64,1024]{1,0:T(8,128)S(1)}, u32[]{:S(2)}, u32[]{:S(2)}) collective-permute-start(f32[64,1024]{1,0:T(8,128)S(1)} %bitcast.319), channel_id=1, source_target_pairs={{1,0},{2,1},{3,2},{4,3},{5,4},{6,5},{7,6},{8,7},{9,8},{10,9},{11,1... | collective-permute-start | bytes 786440 | tf_op jit(solution)/shard_map/ppermute | solution.py:15
  198.6 66.3 %reduce-scatter.5.cloned.1.call-start = ((), (), s32[]{:S(2)}) async-start(), calls=%async_computation.5 | async-start | bytes 1310720 | tf_op jit(solution)/shard_map/reduce_scatter | solution.py:72
  236.2 13.3 %copy-start.3 = (f32[64,1024]{1,0:T(8,128)S(1)}, f32[64,1024]{1,0:T(8,128)}, u32[]{:S(2)}) copy-start(f32[64,1024]{1,0:T(8,128)} %bitcast_add_fusion) | copy-start | bytes 786436
  236.2 13.3 %copy-start.7 = (f32[64,1024]{1,0:T(8,128)S(1)}, f32[64,1024]{1,0:T(8,128)}, u32[]{:S(2)}) copy-start(f32[64,1024]{1,0:T(8,128)} %copy-done.6) | copy-start | bytes 786436
  249.9 61.0 %copy-start.5 = (f32[64,1024]{1,0:T(8,128)S(1)}, f32[64,1024]{1,0:T(8,128)}, u32[]{:S(2)}) copy-start(f32[64,1024]{1,0:T(8,128)} %copy-done.4) | copy-start | bytes 786436
Sparse Core Ops, SparseCore 0:
  39.9 31.8 all-gather.2
  80.9 27.2 reduce-scatter.2
  198.7 29.5 all-gather.4
  237.4 27.3 reduce-scatter.4
where the time goes:
time: 341 us; the launch traced here: 335 us
  waiting for transfers between devices  122 us (36%)
  blocking collectives  79.2 us (23%)
  matrix products  43.8 us (13%)
  other arithmetic  41.8 us (12%)
  local copies, waits for them, and re-layouts  20.9 us (6%)
  between operations  14.7 us (4%)
  starting transfers between devices  12.3 us (4%)
    all_gather x2, waiting for transfers between devices, operate(): piece = lax.all_gather(vector, 'row', axis=1, tiled=True)  54.9 us
    reduce_scatter x2, waiting for transfers between devices, operate(): lax.psum_scatter(partial_rows, 'col', scatter_dimension=1, tiled=True)  40.6 us
    psum x1, blocking collectives, body(): lax.psum((gram_of(precond, residual), gram_of(precond, product), gram_of(...  40 us
    psum x1, blocking collectives, global_sum(): return lax.psum((terms[0], terms[1]), ('row', 'col'))  39.2 us
    ppermute x4, waiting for transfers between devices, shifted(): return lax.ppermute(x, axis, pairs)  26.4 us
    another operation x9, other arithmetic, solve_spd(): factor = jnp.linalg.cholesky(matrix)  19.7 us
    another operation x6, other arithmetic, solve_spd(): return jax.scipy.linalg.cho_solve((factor, True), target)  18 us
    ppermute x4, starting transfers between devices, shifted(): return lax.ppermute(x, axis, pairs)  11.4 us
  transfers between devices with their start and end apart: 8, of which 8 were waited for; matrix products, arithmetic and copies ran while one was open for 7% of the time, Pallas kernels for 0%

commit v1 on v0

v1 whole, which is shorter than its diff:
```python
import functools

import jax
import jax.numpy as jnp
from jax import lax
from jax.experimental import pallas as pl
from jax.experimental.pallas import tpu as pltpu
from jax.sharding import PartitionSpec as P

MESH = pl.DeviceIdType.MESH
F32 = jnp.float32
BF16 = jnp.bfloat16
LOW = 8


def split(x):
    high = x.astype(BF16)
    return high, (x - high.astype(F32)).astype(BF16)


def stacked(x):
    high, low = split(x)
    return jnp.concatenate([high, low], axis=0)


def dot_nt(a, b):
    return lax.dot_general(a, b, (((1,), (1,)), ((), ())), preferred_element_type=F32)


def dot_nn(a, b):
    return lax.dot_general(a, b, (((1,), (0,)), ((), ())), preferred_element_type=F32)


def product3(dot, both, high, low):
    rows = both.shape[0] // 2
    first = dot(both, high)
    return first[:rows] + (first[rows:] + dot(both[:rows], low))


def gram(a, b):
    return lax.dot_general(
        a, b, (((1,), (1,)), ((), ())), precision=lax.Precision.HIGHEST, preferred_element_type=F32
    )


def mixed(coeffs, rows):
    return jnp.dot(coeffs, rows, precision=lax.Precision.HIGHEST, preferred_element_type=F32)


def eliminate(work):
    count = work.shape[0]
    row_ids = lax.broadcasted_iota(jnp.int32, work.shape, 0)
    for k in range(count):
        row = work[k : k + 1, :] / work[k : k + 1, k : k + 1]
        work = jnp.where(row_ids == k, row, work - work[:, k : k + 1] * row)
    return work.T[count:, :]


def kernel(
    rows, cols,
    x_ref, diag_ref, ua_ref, ub_ref, inv_ref, sizes_ref,
    sol_ref, res_ref,
    inv_f32, inv_hi, inv_lo, diag_f32, diag_hi, diag_lo, ua_f32, ub_f32, u_hi, u_lo,
    joined, halo_in, back_out, back_in, spread, vec_z, vec_q, coef_out, coef_in, sum_row, sum_col,
    inv_sem, diag_sem, own_sem, u_send, u_recv, halo_send, halo_recv, back_send, back_recv,
    coef_send, coef_recv, row_send, row_recv, col_send, col_recv,
):
    my_row, my_col = lax.axis_index("row"), lax.axis_index("col")
    total = rows * cols
    me = my_row * cols + my_col
    rhs, tile = x_ref.shape
    spans, reach, span, _ = inv_ref.shape
    halo = (reach - 1) * span
    wide = reach * span

    def coords(device):
        return (device // cols, device % cols)

    following = coords((me + 1) % total)
    previous = coords((me + total - 1) % total)

    barrier = pltpu.get_barrier_semaphore()

    def greet(step, carry):
        pl.semaphore_signal(
            barrier, inc=1, device_id=coords((me + step) % total), device_id_type=MESH
        )
        return carry

    lax.fori_loop(1, total, greet, 0)

    inv_copies = []
    for a in range(spans):
        for t in range(reach):
            copy = pltpu.make_async_copy(
                inv_ref.at[a, t],
                inv_f32.at[a, :, (reach - 1 - t) * span : (reach - t) * span],
                inv_sem.at[a],
            )
            copy.start()
    diag_copy = pltpu.make_async_copy(diag_ref.at[0], diag_f32, diag_sem)
    diag_copy.start()
    ua_rows, ub_rows = ua_ref.shape[1], ub_ref.shape[1]

    def at_rows(ref, index, size):
        return ref.at[pl.ds(pl.multiple_of(index * size, size), size), :]

    own_a = pltpu.make_async_copy(ua_ref.at[my_row], at_rows(ua_f32, my_row, ua_rows), own_sem.at[0])
    own_b = pltpu.make_async_copy(ub_ref.at[my_row], at_rows(ub_f32, my_row, ub_rows), own_sem.at[1])
    own_a.start()
    own_b.start()
    pl.semaphore_wait(barrier, total - 1)

    def remote(src, dst, send, recv, device):
        return pltpu.make_async_remote_copy(
            src_ref=src, dst_ref=dst, send_sem=send, recv_sem=recv, device_id=device,
            device_id_type=MESH,
        )

    def halo_copy(src, call):
        return remote(
            src.at[:, tile - halo : tile], halo_in.at[call], halo_send.at[call],
            halo_recv.at[call], following,
        )

    first_halo = halo_copy(x_ref, 0)
    first_halo.start()

    def send_factors(step, carry):
        peer = (my_row + step) % rows
        remote(ua_ref.at[peer], at_rows(ua_f32, my_row, ua_rows), u_send.at[0, step],
               u_recv.at[0, step], (peer, my_col)).start()
        remote(ub_ref.at[peer], at_rows(ub_f32, my_row, ub_rows), u_send.at[1, step],
               u_recv.at[1, step], (peer, my_col)).start()
        return carry

    lax.fori_loop(1, rows, send_factors, 0)

    subs = sizes_ref.shape[1]
    sizes = jnp.broadcast_to(sizes_ref[...].astype(F32), (subs, subs))
    down = lax.broadcasted_iota(jnp.int32, (subs, subs), 0)
    across = lax.broadcasted_iota(jnp.int32, (subs, subs), 1)
    opening = jnp.sum(jnp.where(across < down, sizes, 0.0), axis=1, keepdims=True)
    behind = (reach - 1) - lax.broadcasted_iota(jnp.int32, (1, wide), 1) // span
    behind = behind.astype(F32)

    vec = x_ref[...]
    joined[:, halo:] = stacked(vec)

    for a in range(spans):
        for t in range(reach):
            pltpu.make_async_copy(
                inv_ref.at[a, t], inv_f32.at[a, :, t * span : (t + 1) * span], inv_sem.at[a]
            ).wait()
        number = (me * spans + a).astype(F32)
        start = jnp.max(jnp.where(opening <= number, opening, 0.0), axis=0, keepdims=True)
        mask = jnp.where(behind <= number - start, 1.0, 0.0)
        high, low = split(inv_f32[a] * mask)
        inv_hi[a] = high
        inv_lo[a] = low

    def forward_own():
        parts = []
        for a in range(spans):
            skip = max(0, halo - a * span)
            parts.append(product3(
                dot_nt, joined[:, a * span + skip : a * span + wide],
                inv_hi[a, :, skip:], inv_lo[a, :, skip:],
            ))
        return parts

    def forward_halo(parts, call):
        joined[:, :halo] = stacked(halo_in[call])
        out = []
        for a in range(spans):
            skip = max(0, halo - a * span)
            part = parts[a]
            if skip:
                part = part + product3(
                    dot_nt, joined[:, a * span : halo], inv_hi[a, :, :skip], inv_lo[a, :, :skip]
                )
            out.append(stacked(part))
        return out

    def backward_halo(forward, call):
        spread[:, :halo] = jnp.zeros((rhs, halo), F32)
        for a in range(spans):
            skip = max(0, halo - a * span)
            if skip:
                spread[:, a * span : halo] += product3(
                    dot_nn, forward[a], inv_hi[a, :, :skip], inv_lo[a, :, :skip]
                )
        back_out[call] = spread[:, :halo]
        copy = remote(back_out.at[call], back_in.at[call], back_send.at[call],
                      back_recv.at[call], previous)
        copy.start()
        return copy

    def backward_own(forward):
        spread[:, halo:] = jnp.zeros((rhs, tile), F32)
        for a in range(spans):
            skip = max(0, halo - a * span)
            spread[:, a * span + skip : a * span + wide] += product3(
                dot_nn, forward[a], inv_hi[a, :, skip:], inv_lo[a, :, skip:]
            )

    def returned(call):
        spread[:, halo + tile - halo :] += back_in[call]
        return spread[:, halo:]

    def send_coeffs(both, call):
        wide_part = dot_nt(u_hi[...], both)
        coeffs = wide_part[:, :rhs] + (wide_part[:, rhs:] + dot_nt(u_lo[...], both[:rhs]))
        half = coeffs.shape[0] // 2
        coef_out[call, :, :rhs] = coeffs[:half]
        coef_out[call, :, rhs:] = coeffs[half:]

        def send(step, carry):
            peer = (me + step) % total
            remote(at_rows(coef_out.at[call], peer, LOW), at_rows(coef_in.at[call], me, LOW),
                   coef_send.at[call], coef_recv.at[call], coords(peer)).start()
            return carry

        lax.fori_loop(1, total, send, 0)
        pltpu.make_async_copy(
            at_rows(coef_out.at[call], me, LOW), at_rows(coef_in.at[call], me, LOW), own_sem.at[2 + call]
        ).start()

    def wait_coeffs(call):
        piece = coef_out.at[call, : (total - 1) * LOW, :]
        pltpu.make_async_copy(piece, piece, coef_recv.at[call]).wait()
        pltpu.make_async_copy(
            at_rows(coef_out.at[call], me, LOW), at_rows(coef_in.at[call], me, LOW), own_sem.at[2 + call]
        ).wait()
        turned = coef_in[call].T
        return stacked(jnp.concatenate([turned[:rhs], turned[rhs:]], axis=1))

    def far_part(call):
        return product3(dot_nn, wait_coeffs(call), u_hi[...], u_lo[...])

    def start_sum(value, call):
        sum_row[call, my_row] = value
        for step in range(1, rows):
            remote(sum_row.at[call, my_row], sum_row.at[call, my_row], row_send.at[call],
                   row_recv.at[call], ((my_row + step) % rows, my_col)).start()

    def middle_sum(call):
        piece = sum_row.at[call, : rows - 1]
        pltpu.make_async_copy(piece, piece, row_recv.at[call]).wait()
        sum_col[call, my_col] = jnp.sum(sum_row[call], axis=0)
        for step in range(1, cols):
            remote(sum_col.at[call, my_col], sum_col.at[call, my_col], col_send.at[call],
                   col_recv.at[call], (my_row, (my_col + step) % cols)).start()

    def end_sum(call):
        piece = sum_col.at[call, : cols - 1]
        pltpu.make_async_copy(piece, piece, col_recv.at[call]).wait()
        return jnp.sum(sum_col[call], axis=0)

    parts = forward_own()
    first_halo.wait_recv()
    forward = forward_halo(parts, 0)
    first_back = backward_halo(forward, 0)
    backward_own(forward)
    diag_copy.wait()

    def split_diag(step, carry):
        where = pl.ds(pl.multiple_of(step * span, span), span)
        high, low = split(diag_f32[where, :])
        diag_hi[where, :] = high
        diag_lo[where, :] = low
        return carry

    lax.fori_loop(0, tile // span, split_diag, 0)
    own_a.wait()
    own_b.wait()

    def wait_factors(step, carry):
        peer = (my_row + step) % rows
        remote(ua_ref.at[peer], at_rows(ua_f32, my_row, ua_rows), u_send.at[0, step],
               u_recv.at[0, step], (peer, my_col)).wait()
        remote(ub_ref.at[peer], at_rows(ub_f32, my_row, ub_rows), u_send.at[1, step],
               u_recv.at[1, step], (peer, my_col)).wait()
        return carry

    lax.fori_loop(1, rows, wait_factors, 0)
    tail = ub_f32.shape[0] // total
    upper = lax.broadcasted_iota(jnp.int32, (LOW, tile), 0) < tail

    def split_factors(step, carry):
        where = pl.ds(pl.multiple_of(step * 2 * LOW, 2 * LOW), 2 * LOW)
        high, low = split(ua_f32[where, :])
        u_hi[where, :] = high
        u_lo[where, :] = low
        pair = ub_f32[pl.ds(pl.multiple_of(step * LOW, LOW), LOW), :]
        other = jnp.concatenate([pair[tail:], pair[:tail]], axis=0)
        both = jnp.concatenate([jnp.where(upper, pair, 0.0), jnp.where(upper, other, 0.0)], axis=0)
        high, low = split(both)
        later = pl.ds(pl.multiple_of(total * LOW + step * 2 * LOW, 2 * LOW), 2 * LOW)
        u_hi[later, :] = high
        u_lo[later, :] = low
        return carry

    lax.fori_loop(0, total // 2, split_factors, 0)
    first_back.wait_recv()
    z0 = returned(0)
    vec_z[...] = z0

    both = stacked(z0)
    send_coeffs(both, 0)
    near = product3(dot_nn, both, diag_hi[...], diag_lo[...])
    q0 = near + far_part(0)
    vec_q[...] = q0
    second_halo = halo_copy(vec_q, 1)
    second_halo.start()

    start_sum(jnp.concatenate([gram(z0, q0), gram(z0, x_ref[...])], axis=1), 0)
    joined[:, halo:] = stacked(q0)
    parts = forward_own()
    middle_sum(0)
    second_halo.wait_recv()
    forward = forward_halo(parts, 1)
    second_back = backward_halo(forward, 1)
    backward_own(forward)
    first_pair = end_sum(0)
    alpha0 = eliminate(first_pair)
    res1 = x_ref[...] - mixed(alpha0, vec_q[...])
    second_back.wait_recv()
    z1 = vec_z[...] - mixed(alpha0, returned(1))

    both = stacked(z1)
    send_coeffs(both, 1)
    start_sum(jnp.concatenate([gram(vec_q[...], z1), gram(z1, res1)], axis=1), 1)
    near = product3(dot_nn, both, diag_hi[...], diag_lo[...])
    middle_sum(1)
    image = near + far_part(1)
    own = gram(z1, image)
    start_sum(jnp.concatenate([own, own], axis=1), 2)
    second_pair = end_sum(1)
    cross, rho1 = second_pair[:, :rhs], second_pair[:, rhs:]
    curve, rho0 = first_pair[:, :rhs], first_pair[:, rhs:]
    beta0_t = eliminate(jnp.concatenate([rho0, rho1], axis=1))
    middle_sum(2)
    search = z1 + mixed(beta0_t, vec_z[...])
    image = image + mixed(beta0_t, vec_q[...])
    sol1 = mixed(alpha0, vec_z[...])
    turned = mixed(beta0_t, cross)
    known = turned + turned.T + gram(mixed(beta0_t, curve), beta0_t)
    own = end_sum(2)[:, :rhs]
    alpha1 = eliminate(jnp.concatenate([own + known, rho1], axis=1))
    sol_ref[...] = sol1 + mixed(alpha1, search)
    res_ref[...] = res1 - mixed(alpha1, image)

    first_halo.wait_send()
    second_halo.wait_send()
    first_back.wait_send()
    second_back.wait_send()
    for call in range(2):
        piece = coef_out.at[call, : (total - 1) * LOW, :]
        pltpu.make_async_copy(piece, piece, coef_send.at[call]).wait()
    for call in range(3):
        piece = sum_row.at[call, : rows - 1]
        pltpu.make_async_copy(piece, piece, row_send.at[call]).wait()
        piece = sum_col.at[call, : cols - 1]
        pltpu.make_async_copy(piece, piece, col_send.at[call]).wait()


def body(rows, cols, right_sides, diag_tiles, low_rank, tile_ranks, inv_factor, sub_sizes):
    rhs, tile = right_sides.shape
    spans, reach, span, _ = inv_factor.shape
    tile_rows, _, groups, _, rank, _ = low_rank.shape
    total = rows * cols
    halo = (reach - 1) * span
    keep = lax.iota(jnp.int32, rank)[None, None, :] < tile_ranks[:, 0, :, None]
    factor = jnp.where(keep[..., None], low_rank[:, 0, :, 1], 0.0).transpose(1, 0, 2, 3)
    ua = factor[:, :, :LOW].reshape(groups, tile_rows * LOW, tile)
    ub = factor[:, :, LOW:].reshape(groups, tile_rows * (rank - LOW), tile)
    anywhere = pl.BlockSpec(memory_space=pl.ANY)
    vmem = pl.BlockSpec(memory_space=pltpu.VMEM)
    dma = pltpu.SemaphoreType.DMA
    out = jax.ShapeDtypeStruct((rhs, tile), F32)
    return pl.pallas_call(
        functools.partial(kernel, rows, cols),
        out_shape=(out, out),
        in_specs=[vmem, anywhere, anywhere, anywhere, anywhere, vmem],
        out_specs=(vmem, vmem),
        scratch_shapes=[
            pltpu.VMEM((spans, span, reach * span), F32),
            pltpu.VMEM((spans, span, reach * span), BF16),
            pltpu.VMEM((spans, span, reach * span), BF16),
            pltpu.VMEM((tile, tile), F32),
            pltpu.VMEM((tile, tile), BF16),
            pltpu.VMEM((tile, tile), BF16),
            pltpu.VMEM((total * LOW, tile), F32),
            pltpu.VMEM((total * (rank - LOW), tile), F32),
            pltpu.VMEM((2 * total * LOW, tile), BF16),
            pltpu.VMEM((2 * total * LOW, tile), BF16),
            pltpu.VMEM((2 * rhs, halo + tile), BF16),
            pltpu.VMEM((2, rhs, halo), F32),
            pltpu.VMEM((2, rhs, halo), F32),
            pltpu.VMEM((2, rhs, halo), F32),
            pltpu.VMEM((rhs, halo + tile), F32),
            pltpu.VMEM((rhs, tile), F32),
            pltpu.VMEM((rhs, tile), F32),
            pltpu.VMEM((2, total * LOW, 2 * rhs), F32),
            pltpu.VMEM((2, total * LOW, 2 * rhs), F32),
            pltpu.VMEM((3, rows, rhs, 2 * rhs), F32),
            pltpu.VMEM((3, cols, rhs, 2 * rhs), F32),
            dma((spans,)), dma, dma((4,)), dma((2, rows)), dma((2, rows)),
            dma((2,)), dma((2,)), dma((2,)), dma((2,)),
            dma((2,)), dma((2,)), dma((3,)), dma((3,)), dma((3,)), dma((3,)),
        ],
        compiler_params=pltpu.CompilerParams(
            collective_id=0, has_side_effects=True, vmem_limit_bytes=60 << 20
        ),
    )(right_sides, diag_tiles, ua, ub, inv_factor, sub_sizes.reshape(1, -1))


def solution(mesh):
    rows, cols = mesh.shape["row"], mesh.shape["col"]
    placed = (
        P(None, ("row", "col")),
        P(("row", "col"), None, None),
        P("row", "col", None, None, None, None),
        P("row", "col", None),
        P(("row", "col"), None, None, None),
        P(),
    )
    return jax.shard_map(
        functools.partial(body, rows, cols),
        mesh=mesh,
        in_specs=placed,
        out_specs=(P(None, ("row", "col")), P(None, ("row", "col"))),
        check_vma=False,
    )
```

time: 341 us -> 94.4 us (0.28); the launches traced: 335 us -> 94.1 us
  waiting for transfers between devices: 122 us -> 0 us
  Pallas kernels: 0 us -> 81.8 us
  blocking collectives: 79.2 us -> 0 us
  matrix products: 43.8 us -> 0 us
  other arithmetic: 41.8 us -> 1.89 us
  between operations: 14.7 us -> 0.67 us
  starting transfers between devices: 12.3 us -> 0 us
  local copies, waits for them, and re-layouts: 20.9 us -> 9.75 us
    pallas_call x0 -> x1, Pallas kernels: none -> 81.8 us  [body(): pl.pallas_call(functools.partial(kernel, rows, cols), out_shape=(out, out...]
    psum x2 -> x0, blocking collectives: 79.2 us -> none  [the longest x1 40 us: body(): lax.psum((gram_of(precond, residual), gram_of(precond, product), gram_of(...]
    all_gather x2 -> x0, waiting for transfers between devices: 54.9 us -> none  [operate(): piece = lax.all_gather(vector, 'row', axis=1, tiled=True)]
    dot_general x25 -> x0, matrix products: 42.6 us -> none  [the longest x2 9.71 us: operate(): local_part = jnp.dot(vector, diag_tiles[0], precision=finest)]
    reduce_scatter x2 -> x0, waiting for transfers between devices: 40.6 us -> none  [operate(): lax.psum_scatter(partial_rows, 'col', scatter_dimension=1, tiled=True)]
    another operation x17 -> x0, other arithmetic: 37.9 us -> none  [the longest x9 19.7 us: solve_spd(): factor = jnp.linalg.cholesky(matrix)]
    ppermute x4 -> x0, waiting for transfers between devices: 26.4 us -> none  [shifted(): return lax.ppermute(x, axis, pairs)]
    ppermute x4 -> x0, starting transfers between devices: 11.4 us -> none  [shifted(): return lax.ppermute(x, axis, pairs)]
  transfers between devices with their start and end apart: 8 -> 0, of which waited for: 8 -> 0; matrix products, arithmetic and copies ran while one was open for 7% -> 0% of each run, Pallas kernels for 0% -> 0%
where the time goes in v1:
time: 94.4 us; the launch traced here: 94.1 us
  Pallas kernels  81.8 us (87%)
  local copies, waits for them, and re-layouts  9.75 us (10%)
  other arithmetic  1.89 us (2%)
    pallas_call x1, Pallas kernels, body(): pl.pallas_call(functools.partial(kernel, rows, cols), out_shape=(out, out...  81.8 us
    slice x1, local copies, waits for them, and re-layouts, body(): low_rank[:, 0, :, 1]  3.54 us
    unnamed x2, local copies, waits for them, and re-layouts  3.34 us

profile of v1, /device:TPU:0, one launch (start us, length us, event | category | flops | bytes accessed | tf_op | source)
XLA Modules:
  0.0 94.1 jit_solution(7395730383279112386)
XLA Ops:
  0.6 0.7 iota_compare_fusion
  1.3 3.5 %slice.9 = f32[4,1,8,1,12,1024]{5,3,4,2,1,0:T(1,128)S(1)} slice(f32[4,1,8,2,12,1024]{5,3,4,2,1,0:T(2,128)} %param.8), slice={[0:4], [0:1], [0:8], [1:2], [0:12], [0:1024]} | slice | bytes 3145728 | tf_op jit(solution)/shard_map/slice | solution.py:375
  4.9 1.2 %fusion.1 = f32[8,4,12,1024]{3,0,2,1:T(8,128)S(1)} fusion(f32[4,1,8,1,12,1024]{5,3,4,2,1,0:T(1,128)S(1)} %slice.9, pred[4,8,12]{1,2,0:T(8,128)(4,1)S(1)} %iota_compare_fusion), kind=kLoop, calls=%fused_computation.2 | loop fusion | flops 393216 | bytes 3146112 | tf_op jit(solution)/shard_map/transpose | solution.py:375
  6.1 0.1 slice.12
  6.2 1.6 %copy.21 = f32[8,4,8,1024]{3,2,1,0:T(8,128)} copy(f32[8,4,8,1024]{3,0,2,1:T(8,128)S(1)} %slice.12) | data formatting | bytes 2097152 | tf_op jit(solution)/shard_map/slice | solution.py:376
  7.8 1.1 %copy.13.ub_ref = f32[8,16,1024]{2,1,0:T(8,128)} copy(f32[8,16,1024]{2,0,1:T(8,128)S(1)} %bitcast.15) | data formatting | bytes 1048576 | tf_op jit(solution)/shard_map/reshape | solution.py:377
  9.0 81.8 %shard_map.77 = (f32[64,1024]{1,0:T(8,128)}, f32[64,1024]{1,0:T(8,128)}) custom-call(f32[64,1024]{1,0:T(8,128)} %x_ref.1, f32[1,1024,1024]{2,1,0:T(8,128)} %diag_ref.1, f32[8,32,1024]{2,1,0:T(8,128)} %bitcast.14, f32[8,16,1024]{2,1,0:T(8,128)} %copy.13.ub_ref, f32[8,8,128,128]{3,2,1,0:T(8,128)} %inv_ref.1, s32[1,64]{1,0:T(1,128)} %bitcast.17), custom_call_target="tpu_custom_call" | custom-call | tf_op jit(solution)/shard_map/pallas_call | solution.py:382
  90.8 1.7 %copy.24 = f32[64,1024]{1,0:T(8,128)} copy(f32[64,1024]{1,0:T(8,128)} %get-tuple-element.4) | data formatting | bytes 524288
  92.4 1.7 %copy.25 = f32[64,1024]{1,0:T(8,128)} copy(f32[64,1024]{1,0:T(8,128)} %get-tuple-element.5) | data formatting | bytes 524288
  (1 shorter events, 0.0 us)

commit v2 on v1

--- a/solution.py
+++ b/solution.py
@@ -11,6 +11,7 @@
 F32 = jnp.float32
 BF16 = jnp.bfloat16
 LOW = 8
+LANES = 128
 
 
 def split(x):
@@ -48,21 +49,44 @@
 
 
 def eliminate(work):
-    count = work.shape[0]
+    count, width = work.shape
+    block = 4
     row_ids = lax.broadcasted_iota(jnp.int32, work.shape, 0)
-    for k in range(count):
-        row = work[k : k + 1, :] / work[k : k + 1, k : k + 1]
-        work = jnp.where(row_ids == k, row, work - work[:, k : k + 1] * row)
-    return work.T[count:, :]
+    for k in range(0, count, block):
+        columns = [jnp.broadcast_to(work[:, k + j : k + j + 1], work.shape) for j in range(block)]
+        rows = [work[k + i : k + i + 1, :] for i in range(block)]
+        heads = [[columns[j][k + i : k + i + 1, :] for j in range(block)] for i in range(block)]
+        for i in range(block):
+            inverse = 1.0 / heads[i][i]
+            rows[i] = rows[i] * inverse
+            for j in range(i + 1, block):
+                heads[i][j] = heads[i][j] * inverse
+            for other in range(block):
+                if other != i:
+                    factor = heads[other][i]
+                    rows[other] = rows[other] - factor * rows[i]
+                    for j in range(i + 1, block):
+                        heads[other][j] = heads[other][j] - factor * heads[i][j]
+        update = columns[0] * rows[0]
+        for j in range(1, block):
+            update = update + columns[j] * rows[j]
+        work = work - update
+        for i in range(block):
+            work = jnp.where(row_ids == k + i, rows[i], work)
+    return work
+
+
+def solved(work):
+    return eliminate(work).T[work.shape[0] :, :]
 
 
 def kernel(
     rows, cols,
-    x_ref, diag_ref, ua_ref, ub_ref, inv_ref, sizes_ref,
+    x_ref, diag_ref, factor_ref, ranks_ref, inv_ref, sizes_ref,
     sol_ref, res_ref,
     inv_f32, inv_hi, inv_lo, diag_f32, diag_hi, diag_lo, ua_f32, ub_f32, u_hi, u_lo,
-    joined, halo_in, back_out, back_in, spread, vec_z, vec_q, coef_out, coef_in, sum_row, sum_col,
-    inv_sem, diag_sem, own_sem, u_send, u_recv, halo_send, halo_recv, back_send, back_recv,
+    factor_f32, pack_a, pack_b, joined, halo_in, back_out, back_in, spread, vec_z, vec_q, coef_out, coef_in, sum_row, sum_col,
+    inv_sem, diag_sem, factor_sem, own_sem, u_send, u_recv, halo_send, halo_recv, back_send, back_recv,
     coef_send, coef_recv, row_send, row_recv, col_send, col_recv,
 ):
     my_row, my_col = lax.axis_index("row"), lax.axis_index("col")
@@ -89,7 +113,8 @@
 
     lax.fori_loop(1, total, greet, 0)
 
-    inv_copies = []
+    factor_copy = pltpu.make_async_copy(factor_ref, factor_f32, factor_sem)
+    factor_copy.start()
     for a in range(spans):
         for t in range(reach):
             copy = pltpu.make_async_copy(
@@ -100,15 +125,49 @@
             copy.start()
     diag_copy = pltpu.make_async_copy(diag_ref.at[0], diag_f32, diag_sem)
     diag_copy.start()
-    ua_rows, ub_rows = ua_ref.shape[1], ub_ref.shape[1]
+    groups = rows
+    rank = factor_ref.shape[0] // (cols * groups * 2 * (tile // LANES))
+    tail = rank - LOW
+    step_rows = 2 * (tile // LANES)
 
     def at_rows(ref, index, size):
         return ref.at[pl.ds(pl.multiple_of(index * size, size), size), :]
 
-    own_a = pltpu.make_async_copy(ua_ref.at[my_row], at_rows(ua_f32, my_row, ua_rows), own_sem.at[0])
-    own_b = pltpu.make_async_copy(ub_ref.at[my_row], at_rows(ub_f32, my_row, ub_rows), own_sem.at[1])
-    own_a.start()
+    def take(base, side, first, size, limit):
+        ids = first + lax.broadcasted_iota(jnp.int32, (size, LANES), 0)
+        pieces = [
+            factor_f32[pl.ds(base + first * step_rows + 2 * i + side, size, stride=step_rows), :]
+            for i in range(tile // LANES)
+        ]
+        return jnp.concatenate([jnp.where(ids < limit, piece, 0.0) for piece in pieces], axis=1)
+
+    factor_copy.wait()
+
+    def pack(k, carry):
+        for a in range(cols):
+            base = (a * groups + k) * rank * step_rows
+            limit = ranks_ref[a, 0, k]
+            pack_a[k, a * LOW : (a + 1) * LOW, :] = take(base, 1, 0, LOW, limit)
+            pack_b[k, a * tail : (a + 1) * tail, :] = take(base, 1, LOW, tail, limit)
+        base = (my_col * groups + k) * rank * step_rows
+        where = pl.ds(pl.multiple_of((k * cols + my_col) * LOW, LOW), LOW)
+        ua_f32[where, :] = take(base, 0, 0, LOW, ranks_ref[my_col, 0, k])
+        return carry
+
+    lax.fori_loop(0, groups, pack, 0)
+    own_b = pltpu.make_async_copy(
+        pack_b.at[my_row], at_rows(ub_f32, my_row, cols * tail), own_sem.at[0]
+    )
     own_b.start()
+
+    def own_a(step):
+        a = (my_col + step) % cols
+        return pltpu.make_async_copy(
+            at_rows(pack_a.at[my_row], a, LOW), at_rows(ua_f32, my_row * cols + a, LOW), own_sem.at[1]
+        )
+
+    for step in range(1, cols):
+        own_a(step).start()
     pl.semaphore_wait(barrier, total - 1)
 
     def remote(src, dst, send, recv, device):
@@ -128,10 +187,12 @@
 
     def send_factors(step, carry):
         peer = (my_row + step) % rows
-        remote(ua_ref.at[peer], at_rows(ua_f32, my_row, ua_rows), u_send.at[0, step],
-               u_recv.at[0, step], (peer, my_col)).start()
-        remote(ub_ref.at[peer], at_rows(ub_f32, my_row, ub_rows), u_send.at[1, step],
-               u_recv.at[1, step], (peer, my_col)).start()
+        for turn in range(1, cols):
+            a = (my_col + turn) % cols
+            remote(at_rows(pack_a.at[peer], a, LOW), at_rows(ua_f32, my_row * cols + a, LOW),
+                   u_send.at[0], u_recv.at[0], (peer, my_col)).start()
+        remote(pack_b.at[peer], at_rows(ub_f32, my_row, cols * tail), u_send.at[1], u_recv.at[1],
+               (peer, my_col)).start()
         return carry
 
     lax.fori_loop(1, rows, send_factors, 0)
@@ -215,13 +276,20 @@
         coef_out[call, :, :rhs] = coeffs[:half]
         coef_out[call, :, rhs:] = coeffs[half:]
 
-        def send(step, carry):
-            peer = (me + step) % total
-            remote(at_rows(coef_out.at[call], peer, LOW), at_rows(coef_in.at[call], me, LOW),
-                   coef_send.at[call], coef_recv.at[call], coords(peer)).start()
+        def send(peer_row, peer_col):
+            remote(at_rows(coef_out.at[call], peer_row * cols + peer_col, LOW),
+                   at_rows(coef_in.at[call], me, LOW),
+                   coef_send.at[call], coef_recv.at[call], (peer_row, peer_col)).start()
+
+        def send_row(step, carry):
+            peer_row = (my_row + step) % rows
+            for turn in range(cols):
+                send(peer_row, (my_col + turn) % cols)
             return carry
 
-        lax.fori_loop(1, total, send, 0)
+        lax.fori_loop(1, rows, send_row, 0)
+        for turn in range(1, cols):
+            send(my_row, (my_col + turn) % cols)
         pltpu.make_async_copy(
             at_rows(coef_out.at[call], me, LOW), at_rows(coef_in.at[call], me, LOW), own_sem.at[2 + call]
         ).start()
@@ -238,24 +306,31 @@
     def far_part(call):
         return product3(dot_nn, wait_coeffs(call), u_hi[...], u_lo[...])
 
+    heights = (rhs, rhs, rhs // 2)
+
     def start_sum(value, call):
-        sum_row[call, my_row] = value
+        high = heights[call]
+        sum_row[call, my_row, :high] = value
         for step in range(1, rows):
-            remote(sum_row.at[call, my_row], sum_row.at[call, my_row], row_send.at[call],
+            mine = sum_row.at[call, my_row, :high]
+            remote(mine, mine, row_send.at[call],
                    row_recv.at[call], ((my_row + step) % rows, my_col)).start()
 
     def middle_sum(call):
-        piece = sum_row.at[call, : rows - 1]
+        high = heights[call]
+        piece = sum_row.at[call, : rows - 1, :high]
         pltpu.make_async_copy(piece, piece, row_recv.at[call]).wait()
-        sum_col[call, my_col] = jnp.sum(sum_row[call], axis=0)
+        sum_col[call, my_col, :high] = jnp.sum(sum_row[call, :, :high], axis=0)
         for step in range(1, cols):
-            remote(sum_col.at[call, my_col], sum_col.at[call, my_col], col_send.at[call],
+            mine = sum_col.at[call, my_col, :high]
+            remote(mine, mine, col_send.at[call],
                    col_recv.at[call], (my_row, (my_col + step) % cols)).start()
 
     def end_sum(call):
-        piece = sum_col.at[call, : cols - 1]
+        high = heights[call]
+        piece = sum_col.at[call, : cols - 1, :high]
         pltpu.make_async_copy(piece, piece, col_recv.at[call]).wait()
-        return jnp.sum(sum_col[call], axis=0)
+        return jnp.sum(sum_col[call, :, :high], axis=0)
 
     parts = forward_own()
     first_halo.wait_recv()
@@ -272,19 +347,13 @@
         return carry
 
     lax.fori_loop(0, tile // span, split_diag, 0)
-    own_a.wait()
     own_b.wait()
-
-    def wait_factors(step, carry):
-        peer = (my_row + step) % rows
-        remote(ua_ref.at[peer], at_rows(ua_f32, my_row, ua_rows), u_send.at[0, step],
-               u_recv.at[0, step], (peer, my_col)).wait()
-        remote(ub_ref.at[peer], at_rows(ub_f32, my_row, ub_rows), u_send.at[1, step],
-               u_recv.at[1, step], (peer, my_col)).wait()
-        return carry
-
-    lax.fori_loop(1, rows, wait_factors, 0)
-    tail = ub_f32.shape[0] // total
+    own_piece = ua_f32.at[: (cols - 1) * LOW, :]
+    pltpu.make_async_copy(own_piece, own_piece, own_sem.at[1]).wait()
+    piece_a = ua_f32.at[: (rows - 1) * (cols - 1) * LOW, :]
+    piece_b = ub_f32.at[: (rows - 1) * cols * tail, :]
+    pltpu.make_async_copy(piece_a, piece_a, u_recv.at[0]).wait()
+    pltpu.make_async_copy(piece_b, piece_b, u_recv.at[1]).wait()
     upper = lax.broadcasted_iota(jnp.int32, (LOW, tile), 0) < tail
 
     def split_factors(step, carry):
@@ -323,7 +392,7 @@
     second_back = backward_halo(forward, 1)
     backward_own(forward)
     first_pair = end_sum(0)
-    alpha0 = eliminate(first_pair)
+    alpha0 = solved(first_pair)
     res1 = x_ref[...] - mixed(alpha0, vec_q[...])
     second_back.wait_recv()
     z1 = vec_z[...] - mixed(alpha0, returned(1))
@@ -332,25 +401,33 @@
     send_coeffs(both, 1)
     start_sum(jnp.concatenate([gram(vec_q[...], z1), gram(z1, res1)], axis=1), 1)
     near = product3(dot_nn, both, diag_hi[...], diag_lo[...])
+    curve, rho0 = first_pair[:, :rhs], first_pair[:, rhs:]
+    square = (rhs, rhs)
+    identity = (
+        lax.broadcasted_iota(jnp.int32, square, 0) == lax.broadcasted_iota(jnp.int32, square, 1)
+    ).astype(F32)
+    inverse = eliminate(jnp.concatenate([rho0, identity], axis=1))[:, rhs:]
+    sol1 = mixed(alpha0, vec_z[...])
     middle_sum(1)
     image = near + far_part(1)
     own = gram(z1, image)
-    start_sum(jnp.concatenate([own, own], axis=1), 2)
+    start_sum(jnp.concatenate([own[: rhs // 2], own[rhs // 2 :]], axis=1), 2)
     second_pair = end_sum(1)
     cross, rho1 = second_pair[:, :rhs], second_pair[:, rhs:]
-    curve, rho0 = first_pair[:, :rhs], first_pair[:, rhs:]
-    beta0_t = eliminate(jnp.concatenate([rho0, rho1], axis=1))
+    beta0_t = mixed(inverse, rho1).T
     middle_sum(2)
     search = z1 + mixed(beta0_t, vec_z[...])
     image = image + mixed(beta0_t, vec_q[...])
-    sol1 = mixed(alpha0, vec_z[...])
     turned = mixed(beta0_t, cross)
     known = turned + turned.T + gram(mixed(beta0_t, curve), beta0_t)
-    own = end_sum(2)[:, :rhs]
-    alpha1 = eliminate(jnp.concatenate([own + known, rho1], axis=1))
+    halves = end_sum(2)
+    own = jnp.concatenate([halves[:, :rhs], halves[:, rhs:]], axis=0)
+    alpha1 = solved(jnp.concatenate([own + known, rho1], axis=1))
     sol_ref[...] = sol1 + mixed(alpha1, search)
     res_ref[...] = res1 - mixed(alpha1, image)
 
+    pltpu.make_async_copy(piece_a, piece_a, u_send.at[0]).wait()
+    pltpu.make_async_copy(piece_b, piece_b, u_send.at[1]).wait()
     first_halo.wait_send()
     second_halo.wait_send()
     first_back.wait_send()
@@ -359,9 +436,9 @@
         piece = coef_out.at[call, : (total - 1) * LOW, :]
         pltpu.make_async_copy(piece, piece, coef_send.at[call]).wait()
     for call in range(3):
-        piece = sum_row.at[call, : rows - 1]
+        piece = sum_row.at[call, : rows - 1, : heights[call]]
         pltpu.make_async_copy(piece, piece, row_send.at[call]).wait()
-        piece = sum_col.at[call, : cols - 1]
+        piece = sum_col.at[call, : cols - 1, : heights[call]]
         pltpu.make_async_copy(piece, piece, col_send.at[call]).wait()
 
 
@@ -371,10 +448,9 @@
     tile_rows, _, groups, _, rank, _ = low_rank.shape
     total = rows * cols
     halo = (reach - 1) * span
-    keep = lax.iota(jnp.int32, rank)[None, None, :] < tile_ranks[:, 0, :, None]
-    factor = jnp.where(keep[..., None], low_rank[:, 0, :, 1], 0.0).transpose(1, 0, 2, 3)
-    ua = factor[:, :, :LOW].reshape(groups, tile_rows * LOW, tile)
-    ub = factor[:, :, LOW:].reshape(groups, tile_rows * (rank - LOW), tile)
+    pieces = tile // LANES
+    factor = low_rank.reshape(tile_rows, groups, 2, rank, pieces, LANES)
+    factor = factor.transpose(0, 1, 3, 4, 2, 5).reshape(-1, LANES)
     anywhere = pl.BlockSpec(memory_space=pl.ANY)
     vmem = pl.BlockSpec(memory_space=pltpu.VMEM)
     dma = pltpu.SemaphoreType.DMA
@@ -382,7 +458,7 @@
     return pl.pallas_call(
         functools.partial(kernel, rows, cols),
         out_shape=(out, out),
-        in_specs=[vmem, anywhere, anywhere, anywhere, anywhere, vmem],
+        in_specs=[vmem, anywhere, anywhere, pl.BlockSpec(memory_space=pltpu.SMEM), anywhere, vmem],
         out_specs=(vmem, vmem),
         scratch_shapes=[
             pltpu.VMEM((spans, span, reach * span), F32),
@@ -395,6 +471,9 @@
             pltpu.VMEM((total * (rank - LOW), tile), F32),
             pltpu.VMEM((2 * total * LOW, tile), BF16),
             pltpu.VMEM((2 * total * LOW, tile), BF16),
+            pltpu.VMEM(factor.shape, F32),
+            pltpu.VMEM((groups, tile_rows * LOW, tile), F32),
+            pltpu.VMEM((groups, tile_rows * (rank - LOW), tile), F32),
             pltpu.VMEM((2 * rhs, halo + tile), BF16),
             pltpu.VMEM((2, rhs, halo), F32),
             pltpu.VMEM((2, rhs, halo), F32),
@@ -406,14 +485,14 @@
             pltpu.VMEM((2, total * LOW, 2 * rhs), F32),
             pltpu.VMEM((3, rows, rhs, 2 * rhs), F32),
             pltpu.VMEM((3, cols, rhs, 2 * rhs), F32),
-            dma((spans,)), dma, dma((4,)), dma((2, rows)), dma((2, rows)),
+            dma((spans,)), dma, dma, dma((4,)), dma((2,)), dma((2,)),
             dma((2,)), dma((2,)), dma((2,)), dma((2,)),
             dma((2,)), dma((2,)), dma((3,)), dma((3,)), dma((3,)), dma((3,)),
         ],
         compiler_params=pltpu.CompilerParams(
             collective_id=0, has_side_effects=True, vmem_limit_bytes=60 << 20
         ),
-    )(right_sides, diag_tiles, ua, ub, inv_factor, sub_sizes.reshape(1, -1))
+    )(right_sides, diag_tiles, factor, tile_ranks, inv_factor, sub_sizes.reshape(1, -1))
 
 
 def solution(mesh):

time: 94.4 us -> 78 us (0.83)
  Pallas kernels: 81.8 us -> 73.9 us
  local copies, waits for them, and re-layouts: 9.75 us -> 3.34 us
  other arithmetic: 1.89 us -> 0 us
    pallas_call x1, Pallas kernels: 81.8 us -> 73.9 us  [body(): pl.pallas_call(functools.partial(kernel, rows, cols), out_shape=(out, out...]
    slice x4 -> x0, local copies, waits for them, and re-layouts: 5.28 us -> none  [the longest x1 3.54 us: body(): low_rank[:, 0, :, 1]]
    transpose x1 -> x0, other arithmetic: 1.2 us -> none  [body(): jnp.where(keep[..., None], low_rank[:, 0, :, 1], 0.0).transpose(1, 0, 2, 3)]
    reshape x1 -> x0, local copies, waits for them, and re-layouts: 1.12 us -> none  [body(): ub = factor[:, :, LOW:].reshape(groups, tile_rows * (rank - LOW), tile)]
where the time goes in v2:
time: 78 us; the launch traced here: 77.8 us
  Pallas kernels  73.9 us (95%)
  local copies, waits for them, and re-layouts  3.34 us (4%)
    pallas_call x1, Pallas kernels, body(): pl.pallas_call(functools.partial(kernel, rows, cols), out_shape=(out, out...  73.9 us
    unnamed x2, local copies, waits for them, and re-layouts  3.34 us

profile of v2, /device:TPU:0, one launch (start us, length us, event | category | flops | bytes accessed | tf_op | source)
XLA Modules:
  0.0 77.8 jit_solution(14086173688660629038)
XLA Ops:
  0.6 73.9 %shard_map.77 = (f32[64,1024]{1,0:T(8,128)}, f32[64,1024]{1,0:T(8,128)}) custom-call(f32[64,1024]{1,0:T(8,128)} %x_ref.1, f32[1,1024,1024]{2,1,0:T(8,128)} %diag_ref.1, f32[6144,128]{1,0:T(8,128)} %bitcast.6, s32[4,1,8]{2,1,0:T(1,128)} %ranks_ref.1, f32[8,8,128,128]{3,2,1,0:T(8,128)} %inv_ref.1, s32[1,64]{1,0:T(1,128)} %bitcast.7), custom_call_target="tpu_custom_call" | custom-call | tf_op jit(solution)/shard_map/pallas_call | solution.py:458
  74.5 1.7 %copy.11 = f32[64,1024]{1,0:T(8,128)} copy(f32[64,1024]{1,0:T(8,128)} %get-tuple-element.4) | data formatting | bytes 524288
  76.2 1.7 %copy.12 = f32[64,1024]{1,0:T(8,128)} copy(f32[64,1024]{1,0:T(8,128)} %get-tuple-element.5) | data formatting | bytes 524288

commit v3 on v2

--- a/solution.py
+++ b/solution.py
@@ -1,4 +1,5 @@
 import functools
+import math
 
 import jax
 import jax.numpy as jnp
@@ -84,8 +85,8 @@
     rows, cols,
     x_ref, diag_ref, factor_ref, ranks_ref, inv_ref, sizes_ref,
     sol_ref, res_ref,
-    inv_f32, inv_hi, inv_lo, diag_f32, diag_hi, diag_lo, ua_f32, ub_f32, u_hi, u_lo,
-    factor_f32, pack_a, pack_b, joined, halo_in, back_out, back_in, spread, vec_z, vec_q, coef_out, coef_in, sum_row, sum_col,
+    inv_f32, inv_hi, inv_lo, diag_f32, diag_hi, diag_lo, u_f32, u_hi, u_lo,
+    factor_f32, packed, joined, halo_in, back_out, back_in, spread, vec_z, vec_q, coef_out, coef_in, sum_row, sum_col,
     inv_sem, diag_sem, factor_sem, own_sem, u_send, u_recv, halo_send, halo_recv, back_send, back_recv,
     coef_send, coef_recv, row_send, row_recv, col_send, col_recv,
 ):
@@ -143,31 +144,31 @@
 
     factor_copy.wait()
 
+    def block(base, side, limit):
+        rest = take(base, side, LOW, tail, limit)
+        rest = jnp.concatenate([rest[:, : tile // 2], rest[:, tile // 2 :]], axis=0)
+        return take(base, side, 0, LOW, limit), rest
+
     def pack(k, carry):
         for a in range(cols):
             base = (a * groups + k) * rank * step_rows
-            limit = ranks_ref[a, 0, k]
-            pack_a[k, a * LOW : (a + 1) * LOW, :] = take(base, 1, 0, LOW, limit)
-            pack_b[k, a * tail : (a + 1) * tail, :] = take(base, 1, LOW, tail, limit)
+            first, rest = block(base, 1, ranks_ref[a, 0, k])
+            packed[k, a * LOW : (a + 1) * LOW, :tile] = first
+            packed[k, a * LOW : (a + 1) * LOW, tile:] = rest
         base = (my_col * groups + k) * rank * step_rows
         where = pl.ds(pl.multiple_of((k * cols + my_col) * LOW, LOW), LOW)
-        ua_f32[where, :] = take(base, 0, 0, LOW, ranks_ref[my_col, 0, k])
+        first, rest = block(base, 0, ranks_ref[my_col, 0, k])
+        u_f32[where, :tile] = first
+        u_f32[where, tile:] = rest
         return carry
 
     lax.fori_loop(0, groups, pack, 0)
-    own_b = pltpu.make_async_copy(
-        pack_b.at[my_row], at_rows(ub_f32, my_row, cols * tail), own_sem.at[0]
-    )
-    own_b.start()
-
-    def own_a(step):
-        a = (my_col + step) % cols
-        return pltpu.make_async_copy(
-            at_rows(pack_a.at[my_row], a, LOW), at_rows(ua_f32, my_row * cols + a, LOW), own_sem.at[1]
-        )
-
-    for step in range(1, cols):
-        own_a(step).start()
+
+    for turn in range(1, cols):
+        a = (my_col + turn) % cols
+        pltpu.make_async_copy(
+            at_rows(packed.at[my_row], a, LOW), at_rows(u_f32, my_row * cols + a, LOW), own_sem.at[1]
+        ).start()
     pl.semaphore_wait(barrier, total - 1)
 
     def remote(src, dst, send, recv, device):
@@ -189,10 +190,8 @@
         peer = (my_row + step) % rows
         for turn in range(1, cols):
             a = (my_col + turn) % cols
-            remote(at_rows(pack_a.at[peer], a, LOW), at_rows(ua_f32, my_row * cols + a, LOW),
-                   u_send.at[0], u_recv.at[0], (peer, my_col)).start()
-        remote(pack_b.at[peer], at_rows(ub_f32, my_row, cols * tail), u_send.at[1], u_recv.at[1],
-               (peer, my_col)).start()
+            remote(at_rows(packed.at[peer], a, LOW), at_rows(u_f32, my_row * cols + a, LOW),
+                   u_send, u_recv, (peer, my_col)).start()
         return carry
 
     lax.fori_loop(1, rows, send_factors, 0)
@@ -306,7 +305,7 @@
     def far_part(call):
         return product3(dot_nn, wait_coeffs(call), u_hi[...], u_lo[...])
 
-    heights = (rhs, rhs, rhs // 2)
+    heights = (rhs // 2, rhs, rhs // 2, rhs // 2)
 
     def start_sum(value, call):
         high = heights[call]
@@ -332,6 +331,12 @@
         pltpu.make_async_copy(piece, piece, col_recv.at[call]).wait()
         return jnp.sum(sum_col[call, :, :high], axis=0)
 
+    def folded(square):
+        return jnp.concatenate([square[: rhs // 2], square[rhs // 2 :]], axis=1)
+
+    def unfolded(halves):
+        return jnp.concatenate([halves[:, :rhs], halves[:, rhs:]], axis=0)
+
     parts = forward_own()
     first_halo.wait_recv()
     forward = forward_halo(parts, 0)
@@ -347,24 +352,25 @@
         return carry
 
     lax.fori_loop(0, tile // span, split_diag, 0)
-    own_b.wait()
-    own_piece = ua_f32.at[: (cols - 1) * LOW, :]
+    own_piece = u_f32.at[: (cols - 1) * LOW, :]
     pltpu.make_async_copy(own_piece, own_piece, own_sem.at[1]).wait()
-    piece_a = ua_f32.at[: (rows - 1) * (cols - 1) * LOW, :]
-    piece_b = ub_f32.at[: (rows - 1) * cols * tail, :]
-    pltpu.make_async_copy(piece_a, piece_a, u_recv.at[0]).wait()
-    pltpu.make_async_copy(piece_b, piece_b, u_recv.at[1]).wait()
-    upper = lax.broadcasted_iota(jnp.int32, (LOW, tile), 0) < tail
+    others = u_f32.at[: (rows - 1) * (cols - 1) * LOW, :]
+    pltpu.make_async_copy(others, others, u_recv).wait()
+    empty = jnp.zeros((LOW - tail, tile), F32)
 
     def split_factors(step, carry):
         where = pl.ds(pl.multiple_of(step * 2 * LOW, 2 * LOW), 2 * LOW)
-        high, low = split(ua_f32[where, :])
+        high, low = split(u_f32[where, :tile])
         u_hi[where, :] = high
         u_lo[where, :] = low
-        pair = ub_f32[pl.ds(pl.multiple_of(step * LOW, LOW), LOW), :]
-        other = jnp.concatenate([pair[tail:], pair[:tail]], axis=0)
-        both = jnp.concatenate([jnp.where(upper, pair, 0.0), jnp.where(upper, other, 0.0)], axis=0)
-        high, low = split(both)
+        rest = u_f32[where, tile:]
+        parts = []
+        for first in (0, LOW):
+            parts.append(jnp.concatenate(
+                [rest[first : first + tail], rest[first + tail : first + 2 * tail]], axis=1
+            ))
+            parts.append(empty)
+        high, low = split(jnp.concatenate(parts, axis=0))
         later = pl.ds(pl.multiple_of(total * LOW + step * 2 * LOW, 2 * LOW), 2 * LOW)
         u_hi[later, :] = high
         u_lo[later, :] = low
@@ -377,13 +383,15 @@
 
     both = stacked(z0)
     send_coeffs(both, 0)
+    start_sum(folded(gram(z0, x_ref[...])), 3)
     near = product3(dot_nn, both, diag_hi[...], diag_lo[...])
+    middle_sum(3)
     q0 = near + far_part(0)
     vec_q[...] = q0
     second_halo = halo_copy(vec_q, 1)
     second_halo.start()
 
-    start_sum(jnp.concatenate([gram(z0, q0), gram(z0, x_ref[...])], axis=1), 0)
+    start_sum(folded(gram(z0, q0)), 0)
     joined[:, halo:] = stacked(q0)
     parts = forward_own()
     middle_sum(0)
@@ -391,8 +399,9 @@
     forward = forward_halo(parts, 1)
     second_back = backward_halo(forward, 1)
     backward_own(forward)
-    first_pair = end_sum(0)
-    alpha0 = solved(first_pair)
+    rho0 = unfolded(end_sum(3))
+    curve = unfolded(end_sum(0))
+    alpha0 = solved(jnp.concatenate([curve, rho0], axis=1))
     res1 = x_ref[...] - mixed(alpha0, vec_q[...])
     second_back.wait_recv()
     z1 = vec_z[...] - mixed(alpha0, returned(1))
@@ -401,7 +410,6 @@
     send_coeffs(both, 1)
     start_sum(jnp.concatenate([gram(vec_q[...], z1), gram(z1, res1)], axis=1), 1)
     near = product3(dot_nn, both, diag_hi[...], diag_lo[...])
-    curve, rho0 = first_pair[:, :rhs], first_pair[:, rhs:]
     square = (rhs, rhs)
     identity = (
         lax.broadcasted_iota(jnp.int32, square, 0) == lax.broadcasted_iota(jnp.int32, square, 1)
@@ -411,7 +419,7 @@
     middle_sum(1)
     image = near + far_part(1)
     own = gram(z1, image)
-    start_sum(jnp.concatenate([own[: rhs // 2], own[rhs // 2 :]], axis=1), 2)
+    start_sum(folded(own), 2)
     second_pair = end_sum(1)
     cross, rho1 = second_pair[:, :rhs], second_pair[:, rhs:]
     beta0_t = mixed(inverse, rho1).T
@@ -420,14 +428,12 @@
     image = image + mixed(beta0_t, vec_q[...])
     turned = mixed(beta0_t, cross)
     known = turned + turned.T + gram(mixed(beta0_t, curve), beta0_t)
-    halves = end_sum(2)
-    own = jnp.concatenate([halves[:, :rhs], halves[:, rhs:]], axis=0)
+    own = unfolded(end_sum(2))
     alpha1 = solved(jnp.concatenate([own + known, rho1], axis=1))
     sol_ref[...] = sol1 + mixed(alpha1, search)
     res_ref[...] = res1 - mixed(alpha1, image)
 
-    pltpu.make_async_copy(piece_a, piece_a, u_send.at[0]).wait()
-    pltpu.make_async_copy(piece_b, piece_b, u_send.at[1]).wait()
+    pltpu.make_async_copy(others, others, u_send).wait()
     first_halo.wait_send()
     second_halo.wait_send()
     first_back.wait_send()
@@ -435,7 +441,7 @@
     for call in range(2):
         piece = coef_out.at[call, : (total - 1) * LOW, :]
         pltpu.make_async_copy(piece, piece, coef_send.at[call]).wait()
-    for call in range(3):
+    for call in range(4):
         piece = sum_row.at[call, : rows - 1, : heights[call]]
         pltpu.make_async_copy(piece, piece, row_send.at[call]).wait()
         piece = sum_col.at[call, : cols - 1, : heights[call]]
@@ -451,46 +457,48 @@
     pieces = tile // LANES
     factor = low_rank.reshape(tile_rows, groups, 2, rank, pieces, LANES)
     factor = factor.transpose(0, 1, 3, 4, 2, 5).reshape(-1, LANES)
-    anywhere = pl.BlockSpec(memory_space=pl.ANY)
+    in_hbm = pl.BlockSpec(memory_space=pltpu.HBM)
     vmem = pl.BlockSpec(memory_space=pltpu.VMEM)
     dma = pltpu.SemaphoreType.DMA
     out = jax.ShapeDtypeStruct((rhs, tile), F32)
+    buffers = [
+        pltpu.VMEM((spans, span, reach * span), F32),
+        pltpu.VMEM((spans, span, reach * span), BF16),
+        pltpu.VMEM((spans, span, reach * span), BF16),
+        pltpu.VMEM((tile, tile), F32),
+        pltpu.VMEM((tile, tile), BF16),
+        pltpu.VMEM((tile, tile), BF16),
+        pltpu.VMEM((total * LOW, tile + tile // 2), F32),
+        pltpu.VMEM((2 * total * LOW, tile), BF16),
+        pltpu.VMEM((2 * total * LOW, tile), BF16),
+        pltpu.VMEM(factor.shape, F32),
+        pltpu.VMEM((groups, tile_rows * LOW, tile + tile // 2), F32),
+        pltpu.VMEM((2 * rhs, halo + tile), BF16),
+        pltpu.VMEM((2, rhs, halo), F32),
+        pltpu.VMEM((2, rhs, halo), F32),
+        pltpu.VMEM((2, rhs, halo), F32),
+        pltpu.VMEM((rhs, halo + tile), F32),
+        pltpu.VMEM((rhs, tile), F32),
+        pltpu.VMEM((rhs, tile), F32),
+        pltpu.VMEM((2, total * LOW, 2 * rhs), F32),
+        pltpu.VMEM((2, total * LOW, 2 * rhs), F32),
+        pltpu.VMEM((4, rows, rhs, 2 * rhs), F32),
+        pltpu.VMEM((4, cols, rhs, 2 * rhs), F32),
+    ]
+    held = sum(math.prod(b.shape) * jnp.dtype(b.dtype).itemsize for b in buffers)
+    grant = min(held + (24 << 20), 62 << 20)
     return pl.pallas_call(
         functools.partial(kernel, rows, cols),
         out_shape=(out, out),
-        in_specs=[vmem, anywhere, anywhere, pl.BlockSpec(memory_space=pltpu.SMEM), anywhere, vmem],
+        in_specs=[vmem, in_hbm, in_hbm, pl.BlockSpec(memory_space=pltpu.SMEM), in_hbm, vmem],
         out_specs=(vmem, vmem),
-        scratch_shapes=[
-            pltpu.VMEM((spans, span, reach * span), F32),
-            pltpu.VMEM((spans, span, reach * span), BF16),
-            pltpu.VMEM((spans, span, reach * span), BF16),
-            pltpu.VMEM((tile, tile), F32),
-            pltpu.VMEM((tile, tile), BF16),
-            pltpu.VMEM((tile, tile), BF16),
-            pltpu.VMEM((total * LOW, tile), F32),
-            pltpu.VMEM((total * (rank - LOW), tile), F32),
-            pltpu.VMEM((2 * total * LOW, tile), BF16),
-            pltpu.VMEM((2 * total * LOW, tile), BF16),
-            pltpu.VMEM(factor.shape, F32),
-            pltpu.VMEM((groups, tile_rows * LOW, tile), F32),
-            pltpu.VMEM((groups, tile_rows * (rank - LOW), tile), F32),
-            pltpu.VMEM((2 * rhs, halo + tile), BF16),
-            pltpu.VMEM((2, rhs, halo), F32),
-            pltpu.VMEM((2, rhs, halo), F32),
-            pltpu.VMEM((2, rhs, halo), F32),
-            pltpu.VMEM((rhs, halo + tile), F32),
-            pltpu.VMEM((rhs, tile), F32),
-            pltpu.VMEM((rhs, tile), F32),
-            pltpu.VMEM((2, total * LOW, 2 * rhs), F32),
-            pltpu.VMEM((2, total * LOW, 2 * rhs), F32),
-            pltpu.VMEM((3, rows, rhs, 2 * rhs), F32),
-            pltpu.VMEM((3, cols, rhs, 2 * rhs), F32),
-            dma((spans,)), dma, dma, dma((4,)), dma((2,)), dma((2,)),
+        scratch_shapes=buffers + [
+            dma((spans,)), dma, dma, dma((4,)), dma, dma,
             dma((2,)), dma((2,)), dma((2,)), dma((2,)),
-            dma((2,)), dma((2,)), dma((3,)), dma((3,)), dma((3,)), dma((3,)),
+            dma((2,)), dma((2,)), dma((4,)), dma((4,)), dma((4,)), dma((4,)),
         ],
         compiler_params=pltpu.CompilerParams(
-            collective_id=0, has_side_effects=True, vmem_limit_bytes=60 << 20
+            collective_id=0, has_side_effects=True, vmem_limit_bytes=grant
         ),
     )(right_sides, diag_tiles, factor, tile_ranks, inv_factor, sub_sizes.reshape(1, -1))
 

time: 78 us -> 75.1 us (0.963)
  Pallas kernels: 73.9 us -> 70.6 us
    pallas_call x1, Pallas kernels: 73.9 us -> 70.6 us  [body(): pl.pallas_call(functools.partial(kernel, rows, cols), out_shape=(out, out...]
    unnamed x2 -> x8, local copies, waits for them, and re-layouts: 3.34 us -> 3.69 us
where the time goes in v3:
time: 75.1 us; the launch traced here: 74.9 us
  Pallas kernels  70.6 us (94%)
  local copies, waits for them, and re-layouts  3.69 us (5%)
    pallas_call x1, Pallas kernels, body(): pl.pallas_call(functools.partial(kernel, rows, cols), out_shape=(out, out...  70.6 us
    unnamed x8, local copies, waits for them, and re-layouts  3.69 us

profile of v3, /device:TPU:0, one launch (start us, length us, event | category | flops | bytes accessed | tf_op | source)
XLA Modules:
  0.0 74.9 jit_solution(3887848990503220488)
XLA Ops:
  0.6 0.0 copy-start
  0.6 0.9 %copy-done = f32[64,1024]{1,0:T(8,128)S(1)} copy-done((f32[64,1024]{1,0:T(8,128)S(1)}, f32[64,1024]{1,0:T(8,128)}, u32[]{:S(2)}) %copy-start) | copy-done | bytes 262168
  1.6 0.0 copy-start.1
  1.6 0.7 copy-done.1
  2.3 0.0 copy-start.2
  2.3 0.7 copy-done.2
  2.9 70.6 %shard_map.77 = (f32[64,1024]{1,0:T(8,128)S(1)}, f32[64,1024]{1,0:T(8,128)S(1)}) custom-call(f32[64,1024]{1,0:T(8,128)S(1)} %copy-done, f32[1,1024,1024]{2,1,0:T(8,128)} %diag_ref.1, f32[6144,128]{1,0:T(8,128)} %bitcast.7, s32[4,1,8]{2,1,0:T(1,128)S(1)} %copy-done.1, f32[8,8,128,128]{3,2,1,0:T(8,128)} %inv_ref.1, s32[1,64]{1,0:T(1,128)S(1)} %bitcast.6), custom_call_target="tpu_custom_call" | custom-call | tf_op jit(solution)/shard_map/pallas_call | solution.py:490
  73.5 0.7 copy.11
  74.2 0.7 copy.12
Async XLA Ops:
  0.6 1.0 %copy-start = (f32[64,1024]{1,0:T(8,128)S(1)}, f32[64,1024]{1,0:T(8,128)}, u32[]{:S(2)}) copy-start(f32[64,1024]{1,0:T(8,128)} %x_ref.1) | copy-start | bytes 786436
  1.6 0.7 copy-start.1
  2.3 0.7 copy-start.2
